TPU v7x, 32 devices: a whole 2x2x4 slice. The times are simulated.
32 devices in a mesh: seq: 16 (over z, y, x), head: 2 (over core).
Axes of the slice: x: 2, y: 2, z: 4, core: 2. Of those that a mesh axis runs over, the one named last changes fastest.
Arguments:
- attn_q: bfloat16 [2048, 512], P('seq', 'head'), may hold values from -6 to 6
- attn_k: bfloat16 [2048, 512], P('seq', 'head'), may hold values from -6 to 6
- attn_v: bfloat16 [2048, 512], P('seq', 'head'), may hold values from -6 to 6
- attn_out: bfloat16 [2048, 512], P('seq', 'head'), may hold values from -0.29882812 to 0.29882812
- attn_dout: bfloat16 [2048, 512], P('seq', 'head'), may hold values from -96 to 96
- attn_lse: float32 [4, 2048], P('head', 'seq'), may hold values from 7 to 8
- w_kv: bfloat16 [512, 2, 512], P('seq', None, 'head'), may hold values from -0.25 to 0.25
- gdn_q: bfloat16 [2048, 512], P('seq', 'head'), may hold values from -6 to 6
- gdn_k: bfloat16 [2048, 512], P('seq', 'head'), may hold values from -6 to 6
- gdn_v: bfloat16 [2048, 512], P('seq', 'head'), may hold values from -6 to 6
- gdn_dout: bfloat16 [2048, 512], P('seq', 'head'), may hold values from -6 to 6
- gdn_log_decay: float32 [4, 2048], P('head', 'seq'), may hold values from -0.56 to 0
- gdn_beta: float32 [4, 2048], P('head', 'seq'), may hold values from 0 to 0.9
- gdn_states: float32 [32, 4, 128, 128], P('seq', 'head'), may hold values from -24 to 24
Outputs:
- attn_dq: bfloat16 [2048, 512], P('seq', 'head')
- attn_dx: bfloat16 [512, 2048], P('head', 'seq')
- gdn_dq: bfloat16 [2048, 512], P('seq', 'head')
- gdn_dk: bfloat16 [2048, 512], P('seq', 'head')
- gdn_dv: bfloat16 [2048, 512], P('seq', 'head')
- gdn_dlog_decay: float32 [4, 2048], P('head', 'seq')
- gdn_dbeta: float32 [4, 2048], P('head', 'seq')
All inputs are finite; a program needn't handle non-finite values.
Results may differ from a plain program's by a relative error of at most 0.0078.
Values may be sent and summed in bfloat16 or wider, within the bound.
A program may use at most 64 MiB of HBM per device.

v0:
```python
import jax
import jax.numpy as jnp
from jax import lax
from jax.sharding import PartitionSpec as P

BLOCK = 64
WINDOW = 1024
HIGH = lax.Precision.HIGHEST


def from_behind(block, axis, distance):
    devices = range(lax.axis_size(axis))
    route = [(i - distance, i) for i in devices if i - distance in devices]
    return lax.ppermute(block, axis, route)


def matmul(left_side, right_side):
    return jnp.dot(left_side, right_side, precision=HIGH)


def stack_mul(left_side, right_side):
    return jnp.einsum("hij,hjk->hik", left_side, right_side, precision=HIGH)


def unit_rows(matrix):
    return matrix * lax.rsqrt(jnp.sum(matrix * matrix, axis=-1, keepdims=True) + 1e-06)


def inverse_unit(lower_part):
    length = lower_part.shape[0]
    identity = jnp.eye(length, dtype=jnp.float32)
    powered = lower_part
    result = identity - lower_part
    for _ in range(length.bit_length() - 2):
        powered = matmul(powered, powered)
        result = matmul(result, identity + powered)
    return result


def block_parts(queries, keys_in, decays, strengths):
    length, depth = queries.shape
    unit_q = unit_rows(queries) * depth ** (-0.5)
    unit_k = unit_rows(keys_in)
    summed = jnp.cumsum(decays)
    row_ids = lax.broadcasted_iota(jnp.int32, (length, length), 0)
    col_ids = lax.broadcasted_iota(jnp.int32, (length, length), 1)
    causal = row_ids >= col_ids
    fading = jnp.where(
        causal, jnp.exp(jnp.where(causal, summed[:, None] - summed[None, :], 0.0)), 0.0
    )
    strict = jnp.where(row_ids > col_ids, fading, 0.0)
    lower_part = strengths[:, None] * strict * matmul(unit_k, unit_k.T)
    solved = inverse_unit(lower_part)
    growth = jnp.exp(summed)
    widened = matmul(solved, (strengths * growth)[:, None] * unit_k)
    attention = fading * matmul(unit_q, unit_k.T)
    tailing = jnp.exp(summed[-1] - summed)[:, None] * unit_k
    return (unit_q, solved, growth, widened, attention, tailing)


def block_forward(queries, keys_in, values, decays, strengths, initial):
    unit_q, solved, growth, widened, attention, tailing = block_parts(
        queries, keys_in, decays, strengths
    )
    fresh = matmul(solved, strengths[:, None] * values) - matmul(widened, initial)
    output = growth[:, None] * matmul(unit_q, initial) + matmul(attention, fresh)
    final = growth[-1] * initial + matmul(tailing.T, fresh)
    return (output, final)


def block_adjoint(queries, keys_in, decays, strengths, out_grad):
    unit_q, solved, growth, widened, attention, tailing = block_parts(
        queries, keys_in, decays, strengths
    )
    depth = queries.shape[1]
    carry_map = growth[-1] * jnp.eye(depth, dtype=jnp.float32) - matmul(widened.T, tailing)
    local_term = matmul((growth[:, None] * unit_q).T, out_grad) - matmul(
        widened.T, matmul(attention.T, out_grad)
    )
    return (carry_map, local_term)


def block_grads(queries, keys_in, values, decays, strengths, initial, out_grad, later_adjoint):
    _, pullback = jax.vjp(block_forward, queries, keys_in, values, decays, strengths, initial)
    grad_q, grad_k, grad_v, grad_decay, grad_beta, _ = pullback((out_grad, later_adjoint))
    return (grad_q, grad_k, grad_v, grad_decay, grad_beta)


def window_terms(queries, keys_in, values, out_grad, log_totals, dot_terms, query_pos, key_pos):
    scaling = queries.shape[2] ** (-0.5)
    logits = (
        jnp.einsum("rhd,khd->hrk", queries, keys_in, preferred_element_type=jnp.float32) * scaling
    )
    distance = query_pos[:, None] - key_pos[None, :]
    visible = ((distance >= 0) & (distance < WINDOW) & (key_pos[None, :] >= 0))[None, :, :]
    chances = jnp.where(
        visible, jnp.exp(jnp.where(visible, logits - log_totals[:, :, None], 0.0)), 0.0
    )
    grad_prob = jnp.einsum("rhd,khd->hrk", out_grad, values, preferred_element_type=jnp.float32)
    grad_logit = (chances * (grad_prob - dot_terms[:, :, None])).astype(jnp.bfloat16)
    weights = chances.astype(jnp.bfloat16)
    grad_q = (
        jnp.einsum("hrk,khd->rhd", grad_logit, keys_in, preferred_element_type=jnp.float32)
        * scaling
    )
    grad_k = (
        jnp.einsum("hrk,rhd->khd", grad_logit, queries, preferred_element_type=jnp.float32)
        * scaling
    )
    grad_v = jnp.einsum("hrk,rhd->khd", weights, out_grad, preferred_element_type=jnp.float32)
    return (grad_q, grad_k, grad_v)


def per_device(
    attn_q,
    attn_k,
    attn_v,
    attn_out,
    attn_dout,
    attn_lse,
    w_kv,
    gdn_q,
    gdn_k,
    gdn_v,
    gdn_dout,
    gdn_log_decay,
    gdn_beta,
    gdn_states,
):
    row_count, column_count = attn_q.shape
    head_count = attn_lse.shape[0]
    depth = column_count // head_count
    reach_count = WINDOW // row_count
    position = lax.axis_index("seq")

    def by_heads(matrix):
        return matrix.reshape(-1, head_count, depth)

    dot_terms = jnp.sum(
        by_heads(attn_dout).astype(jnp.float32) * by_heads(attn_out).astype(jnp.float32), axis=2
    ).T
    query_pos = position * row_count + jnp.arange(row_count, dtype=jnp.int32)
    couple = jnp.stack([attn_k, attn_v])
    pieces = []
    for offset_by in range(reach_count, 0, -1):
        pieces.append(from_behind(couple, "seq", offset_by))
    before = jnp.concatenate(pieces, axis=1)
    window = jnp.concatenate([before, couple], axis=1)
    key_pos = (position - reach_count) * row_count + jnp.arange(
        (reach_count + 1) * row_count, dtype=jnp.int32
    )
    grad_q, grad_k, grad_v = window_terms(
        by_heads(attn_q),
        by_heads(window[0]),
        by_heads(window[1]),
        by_heads(attn_dout),
        attn_lse,
        dot_terms,
        query_pos,
        key_pos,
    )
    own_rows = jnp.stack([attn_q, attn_dout])
    own_stats = jnp.stack([attn_lse, dot_terms])
    query_parts = [own_rows]
    stat_parts = [own_stats]
    for offset_by in range(1, reach_count + 1):
        query_parts.append(from_behind(own_rows, "seq", -offset_by))
        stat_parts.append(from_behind(own_stats, "seq", -offset_by))
    later_rows = jnp.concatenate(query_parts, axis=1)
    later_stats = jnp.concatenate(stat_parts, axis=2)
    later_pos = position * row_count + jnp.arange((reach_count + 1) * row_count, dtype=jnp.int32)
    _, own_k, own_v = window_terms(
        by_heads(later_rows[0]),
        by_heads(attn_k),
        by_heads(attn_v),
        by_heads(later_rows[1]),
        later_stats[0],
        later_stats[1],
        later_pos,
        query_pos,
    )
    key_grad = own_k.reshape(row_count, column_count).astype(jnp.bfloat16)
    value_grad = own_v.reshape(row_count, column_count).astype(jnp.bfloat16)
    attn_dq = grad_q.reshape(row_count, column_count).astype(jnp.bfloat16)
    row_piece = lax.all_gather(w_kv, "seq", axis=0, tiled=True)
    from_keys = lax.dot_general(
        row_piece[:, 0, :], key_grad, (((1,), (1,)), ((), ())), preferred_element_type=jnp.float32
    )
    partial_value = from_keys + lax.dot_general(
        row_piece[:, 1, :], value_grad, (((1,), (1,)), ((), ())), preferred_element_type=jnp.float32
    )
    attn_dx = lax.psum_scatter(partial_value, "head", scatter_dimension=0, tiled=True).astype(
        jnp.bfloat16
    )
    block_count = row_count // BLOCK

    def by_blocks(matrix):
        return (
            matrix.reshape(block_count, BLOCK, head_count, depth)
            .transpose(0, 2, 1, 3)
            .astype(jnp.float32)
        )

    def gates_by_blocks(matrix):
        return matrix.reshape(head_count, block_count, BLOCK).transpose(1, 0, 2)

    queries = by_blocks(gdn_q)
    keys_in = by_blocks(gdn_k)
    values = by_blocks(gdn_v)
    out_grad = by_blocks(gdn_dout)
    decays = gates_by_blocks(gdn_log_decay)
    strengths = gates_by_blocks(gdn_beta)
    carry_map, local_term = jax.vmap(jax.vmap(block_adjoint))(
        queries, keys_in, decays, strengths, out_grad
    )
    identity = jnp.broadcast_to(jnp.eye(depth, dtype=jnp.float32), (head_count, depth, depth))
    nothing = jnp.zeros((head_count, depth, depth), jnp.float32)

    def compose_blocks(carry, couple_in):
        across, offset = carry
        return (
            (stack_mul(couple_in[0], across), stack_mul(couple_in[0], offset) + couple_in[1]),
            None,
        )

    (across, offset), _ = lax.scan(
        compose_blocks, (identity, nothing), (carry_map, local_term), reverse=True
    )

    def relay_step(step_no, incoming):
        return from_behind(stack_mul(across, incoming) + offset, "seq", -1)

    carried = lax.fori_loop(0, lax.axis_size("seq") - 1, relay_step, nothing)

    def backward(carry, couple_in):
        return (stack_mul(couple_in[0], carry) + couple_in[1], carry)

    _, later_adjoint = lax.scan(backward, carried, (carry_map, local_term), reverse=True)
    grad_bq, grad_bk, grad_bv, grad_decay, grad_beta = jax.vmap(jax.vmap(block_grads))(
        queries, keys_in, values, decays, strengths, gdn_states, out_grad, later_adjoint
    )

    def tokens_back(stacked):
        return stacked.transpose(0, 2, 1, 3).reshape(row_count, column_count).astype(jnp.bfloat16)

    def per_head(stacked):
        return stacked.transpose(1, 0, 2).reshape(head_count, row_count)

    return (
        attn_dq,
        attn_dx,
        tokens_back(grad_bq),
        tokens_back(grad_bk),
        tokens_back(grad_bv),
        per_head(grad_decay),
        per_head(grad_beta),
    )


def solution(mesh):
    placed = (
        P("seq", "head"),
        P("seq", "head"),
        P("seq", "head"),
        P("seq", "head"),
        P("seq", "head"),
        P("head", "seq"),
        P("seq", None, "head"),
        P("seq", "head"),
        P("seq", "head"),
        P("seq", "head"),
        P("seq", "head"),
        P("head", "seq"),
        P("head", "seq"),
        P("seq", "head", None, None),
    )
    return jax.shard_map(
        per_device,
        mesh=mesh,
        in_specs=placed,
        out_specs=(
            P("seq", "head"),
            P("head", "seq"),
            P("seq", "head"),
            P("seq", "head"),
            P("seq", "head"),
            P("head", "seq"),
            P("head", "seq"),
        ),
        check_vma=False,
    )
```

profile of v0, /device:TPU:0, one launch (start us, length us, event | category | flops | bytes accessed | tf_op | source)
XLA Modules:
  0.0 311.4 jit_solution(4315394593394781818)
XLA Ops:
  25.4 1.3 fusion.50
  30.9 133.4 %while.43 = (s32[]{:T(128)}, f32[2,128,128]{2,1,0:T(8,128)S(1)}, f32[2,128,128]{2,1,0:T(8,128)S(1)}, f32[2,128,128]{2,1,0:T(8,128)S(1)}, s32[]{:T(128)}) while((s32[]{:T(128)}, f32[2,128,128]{2,1,0:T(8,128)S(1)}, f32[2,128,128]{2,1,0:T(8,128)S(1)}, f32[2,128,128]{2,1,0:T(8,128)S(1)}, s32[]{:T(128)}) %tuple.116), condition=%wide.region_9.10_spmd, body=%wide.region_8.9_spmd.sunk | while | flops 50364416 | bytes 1048677 | solution.py:233
  32.5 7.7 %collective-permute-done = f32[2,128,128]{2,1,0:T(8,128)S(1)} collective-permute-done((f32[2,128,128]{2,1,0:T(8,128)S(1)}, f32[2,128,128]{2,1,0:T(8,128)S(1)}, u32[]{:S(2)}, u32[]{:S(2)}) %collective-permute-start) | collective-permute-done | bytes 131104 | tf_op jit(solution)/shard_map/while/body/eval_jaxpr/ppermute | solution.py:14
  41.8 6.8 %collective-permute-done = f32[2,128,128]{2,1,0:T(8,128)S(1)} collective-permute-done((f32[2,128,128]{2,1,0:T(8,128)S(1)}, f32[2,128,128]{2,1,0:T(8,128)S(1)}, u32[]{:S(2)}, u32[]{:S(2)}) %collective-permute-start) | collective-permute-done | bytes 131104 | tf_op jit(solution)/shard_map/while/body/eval_jaxpr/ppermute | solution.py:14
  48.8 1.3 collective-permute-start
  50.1 6.5 %collective-permute-done = f32[2,128,128]{2,1,0:T(8,128)S(1)} collective-permute-done((f32[2,128,128]{2,1,0:T(8,128)S(1)}, f32[2,128,128]{2,1,0:T(8,128)S(1)}, u32[]{:S(2)}, u32[]{:S(2)}) %collective-permute-start) | collective-permute-done | bytes 131104 | tf_op jit(solution)/shard_map/while/body/eval_jaxpr/ppermute | solution.py:14
  58.2 6.5 %collective-permute-done = f32[2,128,128]{2,1,0:T(8,128)S(1)} collective-permute-done((f32[2,128,128]{2,1,0:T(8,128)S(1)}, f32[2,128,128]{2,1,0:T(8,128)S(1)}, u32[]{:S(2)}, u32[]{:S(2)}) %collective-permute-start) | collective-permute-done | bytes 131104 | tf_op jit(solution)/shard_map/while/body/eval_jaxpr/ppermute | solution.py:14
  66.2 6.9 %collective-permute-done = f32[2,128,128]{2,1,0:T(8,128)S(1)} collective-permute-done((f32[2,128,128]{2,1,0:T(8,128)S(1)}, f32[2,128,128]{2,1,0:T(8,128)S(1)}, u32[]{:S(2)}, u32[]{:S(2)}) %collective-permute-start) | collective-permute-done | bytes 131104 | tf_op jit(solution)/shard_map/while/body/eval_jaxpr/ppermute | solution.py:14
  74.7 7.4 %collective-permute-done = f32[2,128,128]{2,1,0:T(8,128)S(1)} collective-permute-done((f32[2,128,128]{2,1,0:T(8,128)S(1)}, f32[2,128,128]{2,1,0:T(8,128)S(1)}, u32[]{:S(2)}, u32[]{:S(2)}) %collective-permute-start) | collective-permute-done | bytes 131104 | tf_op jit(solution)/shard_map/while/body/eval_jaxpr/ppermute | solution.py:14
  83.6 8.7 %collective-permute-done = f32[2,128,128]{2,1,0:T(8,128)S(1)} collective-permute-done((f32[2,128,128]{2,1,0:T(8,128)S(1)}, f32[2,128,128]{2,1,0:T(8,128)S(1)}, u32[]{:S(2)}, u32[]{:S(2)}) %collective-permute-start) | collective-permute-done | bytes 131104 | tf_op jit(solution)/shard_map/while/body/eval_jaxpr/ppermute | solution.py:14
  93.8 8.7 %collective-permute-done = f32[2,128,128]{2,1,0:T(8,128)S(1)} collective-permute-done((f32[2,128,128]{2,1,0:T(8,128)S(1)}, f32[2,128,128]{2,1,0:T(8,128)S(1)}, u32[]{:S(2)}, u32[]{:S(2)}) %collective-permute-start) | collective-permute-done | bytes 131104 | tf_op jit(solution)/shard_map/while/body/eval_jaxpr/ppermute | solution.py:14
  104.2 7.2 %collective-permute-done = f32[2,128,128]{2,1,0:T(8,128)S(1)} collective-permute-done((f32[2,128,128]{2,1,0:T(8,128)S(1)}, f32[2,128,128]{2,1,0:T(8,128)S(1)}, u32[]{:S(2)}, u32[]{:S(2)}) %collective-permute-start) | collective-permute-done | bytes 131104 | tf_op jit(solution)/shard_map/while/body/eval_jaxpr/ppermute | solution.py:14
  112.9 6.8 %collective-permute-done = f32[2,128,128]{2,1,0:T(8,128)S(1)} collective-permute-done((f32[2,128,128]{2,1,0:T(8,128)S(1)}, f32[2,128,128]{2,1,0:T(8,128)S(1)}, u32[]{:S(2)}, u32[]{:S(2)}) %collective-permute-start) | collective-permute-done | bytes 131104 | tf_op jit(solution)/shard_map/while/body/eval_jaxpr/ppermute | solution.py:14
  121.3 7.1 %collective-permute-done = f32[2,128,128]{2,1,0:T(8,128)S(1)} collective-permute-done((f32[2,128,128]{2,1,0:T(8,128)S(1)}, f32[2,128,128]{2,1,0:T(8,128)S(1)}, u32[]{:S(2)}, u32[]{:S(2)}) %collective-permute-start) | collective-permute-done | bytes 131104 | tf_op jit(solution)/shard_map/while/body/eval_jaxpr/ppermute | solution.py:14
  130.0 7.4 %collective-permute-done = f32[2,128,128]{2,1,0:T(8,128)S(1)} collective-permute-done((f32[2,128,128]{2,1,0:T(8,128)S(1)}, f32[2,128,128]{2,1,0:T(8,128)S(1)}, u32[]{:S(2)}, u32[]{:S(2)}) %collective-permute-start) | collective-permute-done | bytes 131104 | tf_op jit(solution)/shard_map/while/body/eval_jaxpr/ppermute | solution.py:14
  138.9 7.4 %collective-permute-done = f32[2,128,128]{2,1,0:T(8,128)S(1)} collective-permute-done((f32[2,128,128]{2,1,0:T(8,128)S(1)}, f32[2,128,128]{2,1,0:T(8,128)S(1)}, u32[]{:S(2)}, u32[]{:S(2)}) %collective-permute-start) | collective-permute-done | bytes 131104 | tf_op jit(solution)/shard_map/while/body/eval_jaxpr/ppermute | solution.py:14
  147.8 7.4 %collective-permute-done = f32[2,128,128]{2,1,0:T(8,128)S(1)} collective-permute-done((f32[2,128,128]{2,1,0:T(8,128)S(1)}, f32[2,128,128]{2,1,0:T(8,128)S(1)}, u32[]{:S(2)}, u32[]{:S(2)}) %collective-permute-start) | collective-permute-done | bytes 131104 | tf_op jit(solution)/shard_map/while/body/eval_jaxpr/ppermute | solution.py:14
  156.8 7.5 %collective-permute-done = f32[2,128,128]{2,1,0:T(8,128)S(1)} collective-permute-done((f32[2,128,128]{2,1,0:T(8,128)S(1)}, f32[2,128,128]{2,1,0:T(8,128)S(1)}, u32[]{:S(2)}, u32[]{:S(2)}) %collective-permute-start) | collective-permute-done | bytes 131104 | tf_op jit(solution)/shard_map/while/body/eval_jaxpr/ppermute | solution.py:14
  164.3 1.5 collective-permute-start.21
  180.5 54.2 %all_gather.3 = bf16[512,2,256]{2,0,1:T(8,128)(2,1)S(1)} all-gather(bf16[32,2,256]{2,0,1:T(8,128)(2,1)S(1)} %copy.284), channel_id=1, replica_groups=mesh['seq'=16,'head'=2] {'seq'}, dimensions={0}, use_global_device_ids=true | all-gather | bytes 557056 | tf_op jit(solution)/shard_map/all_gather | solution.py:185
  236.6 1.4 fusion.41
  242.9 1.3 collective-permute-start.22
  244.3 1.5 collective-permute-start.23
  257.5 1.9 collective-permute-done.11
  260.7 10.6 %collective-permute-start.1 = (bf16[2,128,256]{1,2,0:T(8,128)(2,1)S(1)}, bf16[2,128,256]{1,2,0:T(8,128)(2,1)}, u32[]{:S(2)}, u32[]{:S(2)}) collective-permute-start(bf16[2,128,256]{1,2,0:T(8,128)(2,1)S(1)} %pad_maximum_fusion), channel_id=1, source_target_pairs={{0,16},{2,18},{4,20},{6,22},{8,24},{10,26},{12,28},{14,30},{1,17},... | collective-permute-start | bytes 393224 | tf_op jit(solution)/shard_map/ppermute | solution.py:14
  271.3 6.4 %collective-permute-start.2 = (bf16[2,128,256]{1,2,0:T(8,128)(2,1)S(1)}, bf16[2,128,256]{1,2,0:T(8,128)(2,1)}, u32[]{:S(2)}, u32[]{:S(2)}) collective-permute-start(bf16[2,128,256]{1,2,0:T(8,128)(2,1)S(1)} %pad_maximum_fusion), channel_id=1, source_target_pairs={{0,14},{2,16},{4,18},{6,20},{8,22},{10,24},{12,26},{14,28},{16,30}... | collective-permute-start | bytes 393224 | tf_op jit(solution)/shard_map/ppermute | solution.py:14
  277.7 1.9 collective-permute-start.3
  279.7 2.0 collective-permute-start.4
  281.7 1.9 collective-permute-start.5
  287.8 3.0 collective-permute-start.6
  291.8 1.3 collective-permute-start.7
  294.0 3.1 collective-permute-start.8
  (307 shorter events, 93.0 us)
Async XLA Ops:
  7.2 295.8 %reduce-scatter.2.cloned.1.call-start = ((), (), s32[]{:S(2)}) async-start(), calls=%async_computation.1 | async-start | bytes 393216 | tf_op jit(solution)/shard_map/reduce_scatter | solution.py:192
  10.0 232.9 %collective-permute-start.17 = (f32[2,2,128]{2,1,0:T(2,128)S(1)}, f32[2,2,128]{2,1,0:T(2,128)S(1)}, u32[]{:S(2)}, u32[]{:S(2)}) collective-permute-start(f32[2,2,128]{2,1,0:T(2,128)S(1)} %get-tuple-element.350), channel_id=1, source_target_pairs={{2,0},{4,2},{6,4},{8,6},{10,8},{12,10},{14,12},{16,14},{18,16},{20... | collective-permute-start | bytes 6152 | tf_op jit(solution)/shard_map/ppermute | solution.py:14
  11.3 233.0 %collective-permute-start.18 = (f32[2,2,128]{2,1,0:T(2,128)S(1)}, f32[2,2,128]{2,1,0:T(2,128)S(1)}, u32[]{:S(2)}, u32[]{:S(2)}) collective-permute-start(f32[2,2,128]{2,1,0:T(2,128)S(1)} %get-tuple-element.350), channel_id=1, source_target_pairs={{4,0},{6,2},{8,4},{10,6},{12,8},{14,10},{16,12},{18,14},{20,16},{2... | collective-permute-start | bytes 6152 | tf_op jit(solution)/shard_map/ppermute | solution.py:14
  12.6 233.2 %collective-permute-start.19 = (f32[2,2,128]{2,1,0:T(2,128)S(1)}, f32[2,2,128]{2,1,0:T(2,128)S(1)}, u32[]{:S(2)}, u32[]{:S(2)}) collective-permute-start(f32[2,2,128]{2,1,0:T(2,128)S(1)} %get-tuple-element.350), channel_id=1, source_target_pairs={{6,0},{8,2},{10,4},{12,6},{14,8},{16,10},{18,12},{20,14},{22,16},{... | collective-permute-start | bytes 6152 | tf_op jit(solution)/shard_map/ppermute | solution.py:14
  13.9 233.2 %collective-permute-start.20 = (f32[2,2,128]{2,1,0:T(2,128)S(1)}, f32[2,2,128]{2,1,0:T(2,128)S(1)}, u32[]{:S(2)}, u32[]{:S(2)}) collective-permute-start(f32[2,2,128]{2,1,0:T(2,128)S(1)} %get-tuple-element.350), channel_id=1, source_target_pairs={{8,0},{10,2},{12,4},{14,6},{16,8},{18,10},{20,12},{22,14},{24,16},... | collective-permute-start | bytes 6152 | tf_op jit(solution)/shard_map/ppermute | solution.py:14
  31.2 9.0 %collective-permute-start = (f32[2,128,128]{2,1,0:T(8,128)S(1)}, f32[2,128,128]{2,1,0:T(8,128)S(1)}, u32[]{:S(2)}, u32[]{:S(2)}) collective-permute-start(f32[2,128,128]{2,1,0:T(8,128)S(1)} %convolution_add_fusion.20), channel_id=1, source_target_pairs={{2,0},{4,2},{6,4},{8,6},{10,8},{12,10},{14,12},{16,14},{18,16},{20... | collective-permute-start | bytes 393224 | tf_op jit(solution)/shard_map/while/body/eval_jaxpr/ppermute | solution.py:14
  40.4 8.1 %collective-permute-start = (f32[2,128,128]{2,1,0:T(8,128)S(1)}, f32[2,128,128]{2,1,0:T(8,128)S(1)}, u32[]{:S(2)}, u32[]{:S(2)}) collective-permute-start(f32[2,128,128]{2,1,0:T(8,128)S(1)} %convolution_add_fusion.20), channel_id=1, source_target_pairs={{2,0},{4,2},{6,4},{8,6},{10,8},{12,10},{14,12},{16,14},{18,16},{20... | collective-permute-start | bytes 393224 | tf_op jit(solution)/shard_map/while/body/eval_jaxpr/ppermute | solution.py:14
  64.9 8.2 %collective-permute-start = (f32[2,128,128]{2,1,0:T(8,128)S(1)}, f32[2,128,128]{2,1,0:T(8,128)S(1)}, u32[]{:S(2)}, u32[]{:S(2)}) collective-permute-start(f32[2,128,128]{2,1,0:T(8,128)S(1)} %convolution_add_fusion.20), channel_id=1, source_target_pairs={{2,0},{4,2},{6,4},{8,6},{10,8},{12,10},{14,12},{16,14},{18,16},{20... | collective-permute-start | bytes 393224 | tf_op jit(solution)/shard_map/while/body/eval_jaxpr/ppermute | solution.py:14
  73.4 8.7 %collective-permute-start = (f32[2,128,128]{2,1,0:T(8,128)S(1)}, f32[2,128,128]{2,1,0:T(8,128)S(1)}, u32[]{:S(2)}, u32[]{:S(2)}) collective-permute-start(f32[2,128,128]{2,1,0:T(8,128)S(1)} %convolution_add_fusion.20), channel_id=1, source_target_pairs={{2,0},{4,2},{6,4},{8,6},{10,8},{12,10},{14,12},{16,14},{18,16},{20... | collective-permute-start | bytes 393224 | tf_op jit(solution)/shard_map/while/body/eval_jaxpr/ppermute | solution.py:14
  82.3 10.0 %collective-permute-start = (f32[2,128,128]{2,1,0:T(8,128)S(1)}, f32[2,128,128]{2,1,0:T(8,128)S(1)}, u32[]{:S(2)}, u32[]{:S(2)}) collective-permute-start(f32[2,128,128]{2,1,0:T(8,128)S(1)} %convolution_add_fusion.20), channel_id=1, source_target_pairs={{2,0},{4,2},{6,4},{8,6},{10,8},{12,10},{14,12},{16,14},{18,16},{20... | collective-permute-start | bytes 393224 | tf_op jit(solution)/shard_map/while/body/eval_jaxpr/ppermute | solution.py:14
  92.5 10.0 %collective-permute-start = (f32[2,128,128]{2,1,0:T(8,128)S(1)}, f32[2,128,128]{2,1,0:T(8,128)S(1)}, u32[]{:S(2)}, u32[]{:S(2)}) collective-permute-start(f32[2,128,128]{2,1,0:T(8,128)S(1)} %convolution_add_fusion.20), channel_id=1, source_target_pairs={{2,0},{4,2},{6,4},{8,6},{10,8},{12,10},{14,12},{16,14},{18,16},{20... | collective-permute-start | bytes 393224 | tf_op jit(solution)/shard_map/while/body/eval_jaxpr/ppermute | solution.py:14
  102.9 8.5 %collective-permute-start = (f32[2,128,128]{2,1,0:T(8,128)S(1)}, f32[2,128,128]{2,1,0:T(8,128)S(1)}, u32[]{:S(2)}, u32[]{:S(2)}) collective-permute-start(f32[2,128,128]{2,1,0:T(8,128)S(1)} %convolution_add_fusion.20), channel_id=1, source_target_pairs={{2,0},{4,2},{6,4},{8,6},{10,8},{12,10},{14,12},{16,14},{18,16},{20... | collective-permute-start | bytes 393224 | tf_op jit(solution)/shard_map/while/body/eval_jaxpr/ppermute | solution.py:14
  111.6 8.1 %collective-permute-start = (f32[2,128,128]{2,1,0:T(8,128)S(1)}, f32[2,128,128]{2,1,0:T(8,128)S(1)}, u32[]{:S(2)}, u32[]{:S(2)}) collective-permute-start(f32[2,128,128]{2,1,0:T(8,128)S(1)} %convolution_add_fusion.20), channel_id=1, source_target_pairs={{2,0},{4,2},{6,4},{8,6},{10,8},{12,10},{14,12},{16,14},{18,16},{20... | collective-permute-start | bytes 393224 | tf_op jit(solution)/shard_map/while/body/eval_jaxpr/ppermute | solution.py:14
  120.0 8.4 %collective-permute-start = (f32[2,128,128]{2,1,0:T(8,128)S(1)}, f32[2,128,128]{2,1,0:T(8,128)S(1)}, u32[]{:S(2)}, u32[]{:S(2)}) collective-permute-start(f32[2,128,128]{2,1,0:T(8,128)S(1)} %convolution_add_fusion.20), channel_id=1, source_target_pairs={{2,0},{4,2},{6,4},{8,6},{10,8},{12,10},{14,12},{16,14},{18,16},{20... | collective-permute-start | bytes 393224 | tf_op jit(solution)/shard_map/while/body/eval_jaxpr/ppermute | solution.py:14
  128.7 8.7 %collective-permute-start = (f32[2,128,128]{2,1,0:T(8,128)S(1)}, f32[2,128,128]{2,1,0:T(8,128)S(1)}, u32[]{:S(2)}, u32[]{:S(2)}) collective-permute-start(f32[2,128,128]{2,1,0:T(8,128)S(1)} %convolution_add_fusion.20), channel_id=1, source_target_pairs={{2,0},{4,2},{6,4},{8,6},{10,8},{12,10},{14,12},{16,14},{18,16},{20... | collective-permute-start | bytes 393224 | tf_op jit(solution)/shard_map/while/body/eval_jaxpr/ppermute | solution.py:14
  137.6 8.7 %collective-permute-start = (f32[2,128,128]{2,1,0:T(8,128)S(1)}, f32[2,128,128]{2,1,0:T(8,128)S(1)}, u32[]{:S(2)}, u32[]{:S(2)}) collective-permute-start(f32[2,128,128]{2,1,0:T(8,128)S(1)} %convolution_add_fusion.20), channel_id=1, source_target_pairs={{2,0},{4,2},{6,4},{8,6},{10,8},{12,10},{14,12},{16,14},{18,16},{20... | collective-permute-start | bytes 393224 | tf_op jit(solution)/shard_map/while/body/eval_jaxpr/ppermute | solution.py:14
  146.5 8.7 %collective-permute-start = (f32[2,128,128]{2,1,0:T(8,128)S(1)}, f32[2,128,128]{2,1,0:T(8,128)S(1)}, u32[]{:S(2)}, u32[]{:S(2)}) collective-permute-start(f32[2,128,128]{2,1,0:T(8,128)S(1)} %convolution_add_fusion.20), channel_id=1, source_target_pairs={{2,0},{4,2},{6,4},{8,6},{10,8},{12,10},{14,12},{16,14},{18,16},{20... | collective-permute-start | bytes 393224 | tf_op jit(solution)/shard_map/while/body/eval_jaxpr/ppermute | solution.py:14
  155.5 8.8 %collective-permute-start = (f32[2,128,128]{2,1,0:T(8,128)S(1)}, f32[2,128,128]{2,1,0:T(8,128)S(1)}, u32[]{:S(2)}, u32[]{:S(2)}) collective-permute-start(f32[2,128,128]{2,1,0:T(8,128)S(1)} %convolution_add_fusion.20), channel_id=1, source_target_pairs={{2,0},{4,2},{6,4},{8,6},{10,8},{12,10},{14,12},{16,14},{18,16},{20... | collective-permute-start | bytes 393224 | tf_op jit(solution)/shard_map/while/body/eval_jaxpr/ppermute | solution.py:14
  164.3 84.2 %collective-permute-start.21 = (f32[2,2,128]{2,1,0:T(2,128)S(1)}, f32[2,2,128]{2,1,0:T(2,128)S(1)}, u32[]{:S(2)}, u32[]{:S(2)}) collective-permute-start(f32[2,2,128]{2,1,0:T(2,128)S(1)} %get-tuple-element.350), channel_id=1, source_target_pairs={{10,0},{12,2},{14,4},{16,6},{18,8},{20,10},{22,12},{24,14},{26,16}... | collective-permute-start | bytes 6152 | tf_op jit(solution)/shard_map/ppermute | solution.py:14
  249.8 9.6 %collective-permute-start.11 = (bf16[2,128,256]{1,2,0:T(8,128)(2,1)S(1)}, bf16[2,128,256]{1,2,0:T(8,128)(2,1)S(1)}, u32[]{:S(2)}, u32[]{:S(2)}) collective-permute-start(bf16[2,128,256]{1,2,0:T(8,128)(2,1)S(1)} %get-tuple-element.334), channel_id=1, source_target_pairs={{6,0},{8,2},{10,4},{12,6},{14,8},{16,10},{18,12},{20,14},{22,16},{... | collective-permute-start | bytes 393224 | tf_op jit(solution)/shard_map/ppermute | solution.py:14
  251.5 9.1 %collective-permute-start.12 = (bf16[2,128,256]{1,2,0:T(8,128)(2,1)S(1)}, bf16[2,128,256]{1,2,0:T(8,128)(2,1)S(1)}, u32[]{:S(2)}, u32[]{:S(2)}) collective-permute-start(bf16[2,128,256]{1,2,0:T(8,128)(2,1)S(1)} %get-tuple-element.334), channel_id=1, source_target_pairs={{8,0},{10,2},{12,4},{14,6},{16,8},{18,10},{20,12},{22,14},{24,16},... | collective-permute-start | bytes 393224 | tf_op jit(solution)/shard_map/ppermute | solution.py:14
  252.8 18.4 %collective-permute-start.13 = (bf16[2,128,256]{1,2,0:T(8,128)(2,1)S(1)}, bf16[2,128,256]{1,2,0:T(8,128)(2,1)S(1)}, u32[]{:S(2)}, u32[]{:S(2)}) collective-permute-start(bf16[2,128,256]{1,2,0:T(8,128)(2,1)S(1)} %get-tuple-element.334), channel_id=1, source_target_pairs={{10,0},{12,2},{14,4},{16,6},{18,8},{20,10},{22,12},{24,14},{26,16}... | collective-permute-start | bytes 393224 | tf_op jit(solution)/shard_map/ppermute | solution.py:14
  254.8 22.9 %collective-permute-start.14 = (bf16[2,128,256]{1,2,0:T(8,128)(2,1)S(1)}, bf16[2,128,256]{1,2,0:T(8,128)(2,1)S(1)}, u32[]{:S(2)}, u32[]{:S(2)}) collective-permute-start(bf16[2,128,256]{1,2,0:T(8,128)(2,1)S(1)} %get-tuple-element.334), channel_id=1, source_target_pairs={{12,0},{14,2},{16,4},{18,6},{20,8},{22,10},{24,12},{26,14},{28,16}... | collective-permute-start | bytes 393224 | tf_op jit(solution)/shard_map/ppermute | solution.py:14
  256.1 23.6 %collective-permute-start.15 = (bf16[2,128,256]{1,2,0:T(8,128)(2,1)S(1)}, bf16[2,128,256]{1,2,0:T(8,128)(2,1)S(1)}, u32[]{:S(2)}, u32[]{:S(2)}) collective-permute-start(bf16[2,128,256]{1,2,0:T(8,128)(2,1)S(1)} %get-tuple-element.334), channel_id=1, source_target_pairs={{14,0},{16,2},{18,4},{20,6},{22,8},{24,10},{26,12},{28,14},{30,16}... | collective-permute-start | bytes 393224 | tf_op jit(solution)/shard_map/ppermute | solution.py:14
  259.3 22.4 %collective-permute-start.16 = (bf16[2,128,256]{1,2,0:T(8,128)(2,1)S(1)}, bf16[2,128,256]{1,2,0:T(8,128)(2,1)S(1)}, u32[]{:S(2)}, u32[]{:S(2)}) collective-permute-start(bf16[2,128,256]{1,2,0:T(8,128)(2,1)S(1)} %get-tuple-element.334), channel_id=1, source_target_pairs={{16,0},{18,2},{20,4},{22,6},{24,8},{26,10},{28,12},{30,14},{17,1},... | collective-permute-start | bytes 393224 | tf_op jit(solution)/shard_map/ppermute | solution.py:14
  260.7 27.2 %collective-permute-start.1 = (bf16[2,128,256]{1,2,0:T(8,128)(2,1)S(1)}, bf16[2,128,256]{1,2,0:T(8,128)(2,1)}, u32[]{:S(2)}, u32[]{:S(2)}) collective-permute-start(bf16[2,128,256]{1,2,0:T(8,128)(2,1)S(1)} %pad_maximum_fusion), channel_id=1, source_target_pairs={{0,16},{2,18},{4,20},{6,22},{8,24},{10,26},{12,28},{14,30},{1,17},... | collective-permute-start | bytes 393224 | tf_op jit(solution)/shard_map/ppermute | solution.py:14
  271.3 20.5 %collective-permute-start.2 = (bf16[2,128,256]{1,2,0:T(8,128)(2,1)S(1)}, bf16[2,128,256]{1,2,0:T(8,128)(2,1)}, u32[]{:S(2)}, u32[]{:S(2)}) collective-permute-start(bf16[2,128,256]{1,2,0:T(8,128)(2,1)S(1)} %pad_maximum_fusion), channel_id=1, source_target_pairs={{0,14},{2,16},{4,18},{6,20},{8,22},{10,24},{12,26},{14,28},{16,30}... | collective-permute-start | bytes 393224 | tf_op jit(solution)/shard_map/ppermute | solution.py:14
  277.7 16.3 %collective-permute-start.3 = (bf16[2,128,256]{1,2,0:T(8,128)(2,1)S(1)}, bf16[2,128,256]{1,2,0:T(8,128)(2,1)}, u32[]{:S(2)}, u32[]{:S(2)}) collective-permute-start(bf16[2,128,256]{1,2,0:T(8,128)(2,1)S(1)} %pad_maximum_fusion), channel_id=1, source_target_pairs={{0,12},{2,14},{4,16},{6,18},{8,20},{10,22},{12,24},{14,26},{16,28}... | collective-permute-start | bytes 393224 | tf_op jit(solution)/shard_map/ppermute | solution.py:14
  279.7 18.4 %collective-permute-start.4 = (bf16[2,128,256]{1,2,0:T(8,128)(2,1)S(1)}, bf16[2,128,256]{1,2,0:T(8,128)(2,1)}, u32[]{:S(2)}, u32[]{:S(2)}) collective-permute-start(bf16[2,128,256]{1,2,0:T(8,128)(2,1)S(1)} %pad_maximum_fusion), channel_id=1, source_target_pairs={{0,10},{2,12},{4,14},{6,16},{8,18},{10,20},{12,22},{14,24},{16,26}... | collective-permute-start | bytes 393224 | tf_op jit(solution)/shard_map/ppermute | solution.py:14
  281.7 17.3 %collective-permute-start.5 = (bf16[2,128,256]{1,2,0:T(8,128)(2,1)S(1)}, bf16[2,128,256]{1,2,0:T(8,128)(2,1)}, u32[]{:S(2)}, u32[]{:S(2)}) collective-permute-start(bf16[2,128,256]{1,2,0:T(8,128)(2,1)S(1)} %pad_maximum_fusion), channel_id=1, source_target_pairs={{0,8},{2,10},{4,12},{6,14},{8,16},{10,18},{12,20},{14,22},{16,24},... | collective-permute-start | bytes 393224 | tf_op jit(solution)/shard_map/ppermute | solution.py:14
  287.8 12.1 %collective-permute-start.6 = (bf16[2,128,256]{1,2,0:T(8,128)(2,1)S(1)}, bf16[2,128,256]{1,2,0:T(8,128)(2,1)S(1)}, u32[]{:S(2)}, u32[]{:S(2)}) collective-permute-start(bf16[2,128,256]{1,2,0:T(8,128)(2,1)S(1)} %pad_maximum_fusion), channel_id=1, source_target_pairs={{0,6},{2,8},{4,10},{6,12},{8,14},{10,16},{12,18},{14,20},{16,22},{... | collective-permute-start | bytes 393224 | tf_op jit(solution)/shard_map/ppermute | solution.py:14
  291.8 8.3 %collective-permute-start.7 = (bf16[2,128,256]{1,2,0:T(8,128)(2,1)S(1)}, bf16[2,128,256]{1,2,0:T(8,128)(2,1)S(1)}, u32[]{:S(2)}, u32[]{:S(2)}) collective-permute-start(bf16[2,128,256]{1,2,0:T(8,128)(2,1)S(1)} %pad_maximum_fusion), channel_id=1, source_target_pairs={{0,4},{2,6},{4,8},{6,10},{8,12},{10,14},{12,16},{14,18},{16,20},{1... | collective-permute-start | bytes 393224 | tf_op jit(solution)/shard_map/ppermute | solution.py:14
  (41 other events, 303.9 us)
Sparse Core Ops, SparseCore 0:
  288.0 4.5 reduce-scatter.1
where the time goes:
time: 313 us; the launch traced here: 311 us
  waiting for transfers between devices  112 us (36%)
  starting transfers between devices  70.6 us (23%)
  blocking collectives  54.2 us (17%)
  matrix products  31.3 us (10%)
  local copies, waits for them, and re-layouts  19.6 us (6%)
  between operations  15.6 us (5%)
  other arithmetic  7.44 us (2%)
    ppermute x39, waiting for transfers between devices, from_behind(): return lax.ppermute(block, axis, route)  112 us
    ppermute x39, starting transfers between devices, from_behind(): return lax.ppermute(block, axis, route)  70.6 us
    all_gather x1, blocking collectives, per_device(): row_piece = lax.all_gather(w_kv, 'seq', axis=0, tiled=True)  54.2 us
    dot_general x53, matrix products, matmul(): return jnp.dot(left_side, right_side, precision=HIGH)  21.9 us
    unnamed x98, local copies, waits for them, and re-layouts  11.8 us
  transfers between devices with their start and end apart: 40, of which 17 were waited for; matrix products, arithmetic and copies ran while one was open for 16% of the time, Pallas kernels for 0%

commit v1 on v0

--- a/solution.py
+++ b/solution.py
@@ -182,7 +182,31 @@
     key_grad = own_k.reshape(row_count, column_count).astype(jnp.bfloat16)
     value_grad = own_v.reshape(row_count, column_count).astype(jnp.bfloat16)
     attn_dq = grad_q.reshape(row_count, column_count).astype(jnp.bfloat16)
-    row_piece = lax.all_gather(w_kv, "seq", axis=0, tiled=True)
+    passed = jax.lax.axis_size("seq")
+    all_rows = jax.lax.axis_index("seq")
+    plain, tmp, out_arr = (passed, all_rows, w_kv.shape[0])
+    by_rank = []
+    for dev, kk in enumerate(w_kv.shape):
+        by_rank.append(kk * plain if dev == 0 else kk)
+    u_next = jnp.zeros(by_rank, w_kv.dtype)
+    row_piece = lax.dynamic_update_slice_in_dim(u_next, w_kv, tmp * out_arr, axis=0)
+    high = back = w_kv
+    for jj in range(1, plain // 2 + 1):
+        seen = []
+        for dev in range(plain):
+            seen.append((dev, (dev + 1) % plain))
+        high = jax.lax.ppermute(high, axis_name="seq", perm=seen)
+        row_piece = lax.dynamic_update_slice_in_dim(
+            row_piece, high, (tmp - jj) % plain * out_arr, axis=0
+        )
+        if 2 * jj < plain:
+            gallery = []
+            for dev in range(plain):
+                gallery.append((dev, (dev - 1) % plain))
+            back = jax.lax.ppermute(back, "seq", gallery)
+            row_piece = lax.dynamic_update_slice_in_dim(
+                row_piece, back, (tmp + jj) % plain * out_arr, axis=0
+            )
     from_keys = lax.dot_general(
         row_piece[:, 0, :], key_grad, (((1,), (1,)), ((), ())), preferred_element_type=jnp.float32
     )

time: 313 us -> 346 us (1.11)
  blocking collectives: 54.2 us -> 0 us
  waiting for transfers between devices: 112 us -> 163 us
  starting transfers between devices: 70.6 us -> 97.6 us
  other arithmetic: 7.44 us -> 12 us
    all_gather x1 -> x0, blocking collectives: 54.2 us -> none  [per_device(): row_piece = lax.all_gather(w_kv, 'seq', axis=0, tiled=True)]
    ppermute x0 -> x15, waiting for transfers between devices: none -> 39.2 us  [the longest x8 32.5 us: per_device(): high = jax.lax.ppermute(high, axis_name='seq', perm=seen)]
    ppermute x0 -> x15, starting transfers between devices: none -> 31.7 us  [the longest x7 26 us: per_device(): back = jax.lax.ppermute(back, 'seq', gallery)]
    ppermute x39, waiting for transfers between devices: 112 us -> 122 us  [from_behind(): return lax.ppermute(block, axis, route)]
    ppermute x39, starting transfers between devices: 70.6 us -> 65.9 us  [from_behind(): return lax.ppermute(block, axis, route)]
    dynamic_update_slice x0 -> x15, local copies, waits for them, and re-layouts: none -> 4.63 us  [the longest x7 2.31 us: per_device(): lax.dynamic_update_slice_in_dim(row_piece, back, (tmp + jj) % plain * out...]
    unnamed x98 -> x157, local copies, waits for them, and re-layouts: 11.8 us -> 10.3 us
  transfers between devices with their start and end apart: 40 -> 55, of which waited for: 17 -> 29; matrix products, arithmetic and copies ran while one was open for 16% -> 17% of each run, Pallas kernels for 0% -> 0%
where the time goes in v1:
time: 346 us; the launch traced here: 344 us
  waiting for transfers between devices  163 us (47%)
  starting transfers between devices  97.6 us (28%)
  matrix products  34.4 us (10%)
  local copies, waits for them, and re-layouts  20 us (6%)
  between operations  16 us (5%)
  other arithmetic  12 us (3%)
    ppermute x39, waiting for transfers between devices, from_behind(): return lax.ppermute(block, axis, route)  122 us
    ppermute x39, starting transfers between devices, from_behind(): return lax.ppermute(block, axis, route)  65.9 us
    ppermute x8, waiting for transfers between devices, per_device(): high = jax.lax.ppermute(high, axis_name='seq', perm=seen)  32.5 us
    ppermute x7, starting transfers between devices, per_device(): back = jax.lax.ppermute(back, 'seq', gallery)  26 us
    dot_general x53, matrix products, matmul(): return jnp.dot(left_side, right_side, precision=HIGH)  23.5 us
    unnamed x157, local copies, waits for them, and re-layouts  10.3 us
  transfers between devices with their start and end apart: 55, of which 29 were waited for; matrix products, arithmetic and copies ran while one was open for 17% of the time, Pallas kernels for 0%

profile of v1, /device:TPU:0, one launch (start us, length us, event | category | flops | bytes accessed | tf_op | source)
XLA Modules:
  0.0 343.7 jit_solution(11903863473928804057)
XLA Ops:
  11.7 4.0 %collective-permute-start.10 = (bf16[32,2,256]{2,0,1:T(8,128)(2,1)}, bf16[32,2,256]{2,0,1:T(8,128)(2,1)}, u32[]{:S(2)}, u32[]{:S(2)}) collective-permute-start(bf16[32,2,256]{2,0,1:T(8,128)(2,1)} %get-tuple-element.336), channel_id=1, source_target_pairs={{0,30},{2,0},{4,2},{6,4},{8,6},{10,8},{12,10},{14,12},{16,14},{18,... | collective-permute-start | bytes 98312 | tf_op jit(solution)/shard_map/ppermute | solution.py:206
  37.0 132.2 %while.43 = (s32[]{:T(128)}, f32[2,128,128]{2,1,0:T(8,128)S(1)}, f32[2,128,128]{2,1,0:T(8,128)S(1)}, f32[2,128,128]{2,1,0:T(8,128)S(1)}, s32[]{:T(128)}) while((s32[]{:T(128)}, f32[2,128,128]{2,1,0:T(8,128)S(1)}, f32[2,128,128]{2,1,0:T(8,128)S(1)}, f32[2,128,128]{2,1,0:T(8,128)S(1)}, s32[]{:T(128)}) %tuple.117), condition=%wide.region_9.10_spmd, body=%wide.region_8.9_spmd.sunk | while | flops 50364416 | bytes 1048677 | solution.py:257
  38.6 6.2 %collective-permute-done = f32[2,128,128]{2,1,0:T(8,128)S(1)} collective-permute-done((f32[2,128,128]{2,1,0:T(8,128)S(1)}, f32[2,128,128]{2,1,0:T(8,128)S(1)}, u32[]{:S(2)}, u32[]{:S(2)}) %collective-permute-start) | collective-permute-done | bytes 131104 | tf_op jit(solution)/shard_map/while/body/eval_jaxpr/ppermute | solution.py:14
  46.3 6.5 %collective-permute-done = f32[2,128,128]{2,1,0:T(8,128)S(1)} collective-permute-done((f32[2,128,128]{2,1,0:T(8,128)S(1)}, f32[2,128,128]{2,1,0:T(8,128)S(1)}, u32[]{:S(2)}, u32[]{:S(2)}) %collective-permute-start) | collective-permute-done | bytes 131104 | tf_op jit(solution)/shard_map/while/body/eval_jaxpr/ppermute | solution.py:14
  54.4 6.5 %collective-permute-done = f32[2,128,128]{2,1,0:T(8,128)S(1)} collective-permute-done((f32[2,128,128]{2,1,0:T(8,128)S(1)}, f32[2,128,128]{2,1,0:T(8,128)S(1)}, u32[]{:S(2)}, u32[]{:S(2)}) %collective-permute-start) | collective-permute-done | bytes 131104 | tf_op jit(solution)/shard_map/while/body/eval_jaxpr/ppermute | solution.py:14
  62.4 6.5 %collective-permute-done = f32[2,128,128]{2,1,0:T(8,128)S(1)} collective-permute-done((f32[2,128,128]{2,1,0:T(8,128)S(1)}, f32[2,128,128]{2,1,0:T(8,128)S(1)}, u32[]{:S(2)}, u32[]{:S(2)}) %collective-permute-start) | collective-permute-done | bytes 131104 | tf_op jit(solution)/shard_map/while/body/eval_jaxpr/ppermute | solution.py:14
  70.4 6.5 %collective-permute-done = f32[2,128,128]{2,1,0:T(8,128)S(1)} collective-permute-done((f32[2,128,128]{2,1,0:T(8,128)S(1)}, f32[2,128,128]{2,1,0:T(8,128)S(1)}, u32[]{:S(2)}, u32[]{:S(2)}) %collective-permute-start) | collective-permute-done | bytes 131104 | tf_op jit(solution)/shard_map/while/body/eval_jaxpr/ppermute | solution.py:14
  78.5 7.9 %collective-permute-done = f32[2,128,128]{2,1,0:T(8,128)S(1)} collective-permute-done((f32[2,128,128]{2,1,0:T(8,128)S(1)}, f32[2,128,128]{2,1,0:T(8,128)S(1)}, u32[]{:S(2)}, u32[]{:S(2)}) %collective-permute-start) | collective-permute-done | bytes 131104 | tf_op jit(solution)/shard_map/while/body/eval_jaxpr/ppermute | solution.py:14
  88.0 8.8 %collective-permute-done = f32[2,128,128]{2,1,0:T(8,128)S(1)} collective-permute-done((f32[2,128,128]{2,1,0:T(8,128)S(1)}, f32[2,128,128]{2,1,0:T(8,128)S(1)}, u32[]{:S(2)}, u32[]{:S(2)}) %collective-permute-start) | collective-permute-done | bytes 131104 | tf_op jit(solution)/shard_map/while/body/eval_jaxpr/ppermute | solution.py:14
  98.4 7.9 %collective-permute-done = f32[2,128,128]{2,1,0:T(8,128)S(1)} collective-permute-done((f32[2,128,128]{2,1,0:T(8,128)S(1)}, f32[2,128,128]{2,1,0:T(8,128)S(1)}, u32[]{:S(2)}, u32[]{:S(2)}) %collective-permute-start) | collective-permute-done | bytes 131104 | tf_op jit(solution)/shard_map/while/body/eval_jaxpr/ppermute | solution.py:14
  107.8 7.5 %collective-permute-done = f32[2,128,128]{2,1,0:T(8,128)S(1)} collective-permute-done((f32[2,128,128]{2,1,0:T(8,128)S(1)}, f32[2,128,128]{2,1,0:T(8,128)S(1)}, u32[]{:S(2)}, u32[]{:S(2)}) %collective-permute-start) | collective-permute-done | bytes 131104 | tf_op jit(solution)/shard_map/while/body/eval_jaxpr/ppermute | solution.py:14
  116.9 6.8 %collective-permute-done = f32[2,128,128]{2,1,0:T(8,128)S(1)} collective-permute-done((f32[2,128,128]{2,1,0:T(8,128)S(1)}, f32[2,128,128]{2,1,0:T(8,128)S(1)}, u32[]{:S(2)}, u32[]{:S(2)}) %collective-permute-start) | collective-permute-done | bytes 131104 | tf_op jit(solution)/shard_map/while/body/eval_jaxpr/ppermute | solution.py:14
  125.3 7.4 %collective-permute-done = f32[2,128,128]{2,1,0:T(8,128)S(1)} collective-permute-done((f32[2,128,128]{2,1,0:T(8,128)S(1)}, f32[2,128,128]{2,1,0:T(8,128)S(1)}, u32[]{:S(2)}, u32[]{:S(2)}) %collective-permute-start) | collective-permute-done | bytes 131104 | tf_op jit(solution)/shard_map/while/body/eval_jaxpr/ppermute | solution.py:14
  134.2 7.4 %collective-permute-done = f32[2,128,128]{2,1,0:T(8,128)S(1)} collective-permute-done((f32[2,128,128]{2,1,0:T(8,128)S(1)}, f32[2,128,128]{2,1,0:T(8,128)S(1)}, u32[]{:S(2)}, u32[]{:S(2)}) %collective-permute-start) | collective-permute-done | bytes 131104 | tf_op jit(solution)/shard_map/while/body/eval_jaxpr/ppermute | solution.py:14
  143.2 7.6 %collective-permute-done = f32[2,128,128]{2,1,0:T(8,128)S(1)} collective-permute-done((f32[2,128,128]{2,1,0:T(8,128)S(1)}, f32[2,128,128]{2,1,0:T(8,128)S(1)}, u32[]{:S(2)}, u32[]{:S(2)}) %collective-permute-start) | collective-permute-done | bytes 131104 | tf_op jit(solution)/shard_map/while/body/eval_jaxpr/ppermute | solution.py:14
  152.3 7.6 %collective-permute-done = f32[2,128,128]{2,1,0:T(8,128)S(1)} collective-permute-done((f32[2,128,128]{2,1,0:T(8,128)S(1)}, f32[2,128,128]{2,1,0:T(8,128)S(1)}, u32[]{:S(2)}, u32[]{:S(2)}) %collective-permute-start) | collective-permute-done | bytes 131104 | tf_op jit(solution)/shard_map/while/body/eval_jaxpr/ppermute | solution.py:14
  161.6 7.6 %collective-permute-done = f32[2,128,128]{2,1,0:T(8,128)S(1)} collective-permute-done((f32[2,128,128]{2,1,0:T(8,128)S(1)}, f32[2,128,128]{2,1,0:T(8,128)S(1)}, u32[]{:S(2)}, u32[]{:S(2)}) %collective-permute-start) | collective-permute-done | bytes 131104 | tf_op jit(solution)/shard_map/while/body/eval_jaxpr/ppermute | solution.py:14
  204.1 5.3 %collective-permute-done.35 = f32[2,2,128]{2,1,0:T(2,128)S(1)} collective-permute-done((f32[2,2,128]{2,1,0:T(2,128)}, f32[2,2,128]{2,1,0:T(2,128)S(1)}, u32[]{:S(2)}, u32[]{:S(2)}) %collective-permute-start.35) | collective-permute-done | bytes 2080 | tf_op jit(solution)/shard_map/ppermute | solution.py:14
  210.7 3.2 collective-permute-done.36
  215.2 3.6 %collective-permute-done.37 = f32[2,2,128]{2,1,0:T(2,128)S(1)} collective-permute-done((f32[2,2,128]{2,1,0:T(2,128)}, f32[2,2,128]{2,1,0:T(2,128)S(1)}, u32[]{:S(2)}, u32[]{:S(2)}) %collective-permute-start.37) | collective-permute-done | bytes 2080 | tf_op jit(solution)/shard_map/ppermute | solution.py:14
  228.7 13.1 %collective-permute-done.11 = bf16[32,2,256]{2,0,1:T(8,128)(2,1)S(1)} collective-permute-done((bf16[32,2,256]{2,0,1:T(8,128)(2,1)}, bf16[32,2,256]{2,0,1:T(8,128)(2,1)S(1)}, u32[]{:S(2)}, u32[]{:S(2)}) %collective-permute-start.11) | collective-permute-done | bytes 32800 | tf_op jit(solution)/shard_map/ppermute | solution.py:198
  242.1 3.8 %collective-permute-done.12 = bf16[32,2,256]{2,0,1:T(8,128)(2,1)S(1)} collective-permute-done((bf16[32,2,256]{2,0,1:T(8,128)(2,1)}, bf16[32,2,256]{2,0,1:T(8,128)(2,1)S(1)}, u32[]{:S(2)}, u32[]{:S(2)}) %collective-permute-start.12) | collective-permute-done | bytes 32800 | tf_op jit(solution)/shard_map/ppermute | solution.py:206
  245.9 7.6 %collective-permute-done.13 = bf16[32,2,256]{2,0,1:T(8,128)(2,1)} collective-permute-done((bf16[32,2,256]{2,0,1:T(8,128)(2,1)S(1)}, bf16[32,2,256]{2,0,1:T(8,128)(2,1)}, u32[]{:S(2)}, u32[]{:S(2)}) %collective-permute-start.13) | collective-permute-done | bytes 32800 | tf_op jit(solution)/shard_map/ppermute | solution.py:198
  263.7 5.5 %collective-permute-start.1 = (bf16[2,128,256]{1,2,0:T(8,128)(2,1)}, bf16[2,128,256]{1,2,0:T(8,128)(2,1)S(1)}, u32[]{:S(2)}, u32[]{:S(2)}) collective-permute-start(bf16[2,128,256]{1,2,0:T(8,128)(2,1)} %pad_maximum_fusion), channel_id=1, source_target_pairs={{0,16},{2,18},{4,20},{6,22},{8,24},{10,26},{12,28},{14,30},{1,17},... | collective-permute-start | bytes 393224 | tf_op jit(solution)/shard_map/ppermute | solution.py:14
  269.2 6.4 %collective-permute-start.2 = (bf16[2,128,256]{1,2,0:T(8,128)(2,1)}, bf16[2,128,256]{1,2,0:T(8,128)(2,1)S(1)}, u32[]{:S(2)}, u32[]{:S(2)}) collective-permute-start(bf16[2,128,256]{1,2,0:T(8,128)(2,1)} %pad_maximum_fusion), channel_id=1, source_target_pairs={{0,14},{2,16},{4,18},{6,20},{8,22},{10,24},{12,26},{14,28},{16,30}... | collective-permute-start | bytes 393224 | tf_op jit(solution)/shard_map/ppermute | solution.py:14
  281.0 3.9 %collective-permute-start.6 = (bf16[2,128,256]{1,2,0:T(8,128)(2,1)}, bf16[2,128,256]{1,2,0:T(8,128)(2,1)S(1)}, u32[]{:S(2)}, u32[]{:S(2)}) collective-permute-start(bf16[2,128,256]{1,2,0:T(8,128)(2,1)} %pad_maximum_fusion), channel_id=1, source_target_pairs={{0,6},{2,8},{4,10},{6,12},{8,14},{10,16},{12,18},{14,20},{16,22},{... | collective-permute-start | bytes 393224 | tf_op jit(solution)/shard_map/ppermute | solution.py:14
  286.5 3.5 %collective-permute-start.8 = (bf16[2,128,256]{1,2,0:T(8,128)(2,1)}, bf16[2,128,256]{1,2,0:T(8,128)(2,1)S(1)}, u32[]{:S(2)}, u32[]{:S(2)}) collective-permute-start(bf16[2,128,256]{1,2,0:T(8,128)(2,1)} %pad_maximum_fusion), channel_id=1, source_target_pairs={{0,2},{2,4},{4,6},{6,8},{8,10},{10,12},{12,14},{14,16},{16,18},{18... | collective-permute-start | bytes 393224 | tf_op jit(solution)/shard_map/ppermute | solution.py:14
  291.3 4.5 %collective-permute-start.16 = (bf16[32,2,256]{2,0,1:T(8,128)(2,1)}, bf16[32,2,256]{2,0,1:T(8,128)(2,1)}, u32[]{:S(2)}, u32[]{:S(2)}) collective-permute-start(bf16[32,2,256]{2,0,1:T(8,128)(2,1)} %collective-permute-done.14), channel_id=1, source_target_pairs={{0,30},{2,0},{4,2},{6,4},{8,6},{10,8},{12,10},{14,12},{16,14},{18,... | collective-permute-start | bytes 98312 | tf_op jit(solution)/shard_map/ppermute | solution.py:206
  300.2 5.6 %collective-permute-start.18 = (bf16[32,2,256]{2,0,1:T(8,128)(2,1)}, bf16[32,2,256]{2,0,1:T(8,128)(2,1)S(1)}, u32[]{:S(2)}, u32[]{:S(2)}) collective-permute-start(bf16[32,2,256]{2,0,1:T(8,128)(2,1)} %collective-permute-done.16), channel_id=1, source_target_pairs={{0,30},{2,0},{4,2},{6,4},{8,6},{10,8},{12,10},{14,12},{16,14},{18,... | collective-permute-start | bytes 98312 | tf_op jit(solution)/shard_map/ppermute | solution.py:206
  307.9 5.6 %collective-permute-start.20 = (bf16[32,2,256]{2,0,1:T(8,128)(2,1)S(1)}, bf16[32,2,256]{2,0,1:T(8,128)(2,1)S(1)}, u32[]{:S(2)}, u32[]{:S(2)}) collective-permute-start(bf16[32,2,256]{2,0,1:T(8,128)(2,1)S(1)} %collective-permute-done.18), channel_id=1, source_target_pairs={{0,30},{2,0},{4,2},{6,4},{8,6},{10,8},{12,10},{14,12},{16,14},{18,... | collective-permute-start | bytes 98312 | tf_op jit(solution)/shard_map/ppermute | solution.py:206
  315.4 5.6 %collective-permute-start.22 = (bf16[32,2,256]{2,0,1:T(8,128)(2,1)S(1)}, bf16[32,2,256]{2,0,1:T(8,128)(2,1)S(1)}, u32[]{:S(2)}, u32[]{:S(2)}) collective-permute-start(bf16[32,2,256]{2,0,1:T(8,128)(2,1)S(1)} %collective-permute-done.20), channel_id=1, source_target_pairs={{0,30},{2,0},{4,2},{6,4},{8,6},{10,8},{12,10},{14,12},{16,14},{18,... | collective-permute-start | bytes 98312 | tf_op jit(solution)/shard_map/ppermute | solution.py:206
  322.9 7.5 %collective-permute-done.23 = bf16[32,2,256]{2,0,1:T(8,128)(2,1)S(1)} collective-permute-done((bf16[32,2,256]{2,0,1:T(8,128)(2,1)S(1)}, bf16[32,2,256]{2,0,1:T(8,128)(2,1)S(1)}, u32[]{:S(2)}, u32[]{:S(2)}) %collective-permute-start.23) | collective-permute-done | bytes 32800 | tf_op jit(solution)/shard_map/ppermute | solution.py:198
  (411 shorter events, 132.0 us)
Async XLA Ops:
  7.2 328.1 %reduce-scatter.2.cloned.1.call-start = ((), (), s32[]{:S(2)}) async-start(), calls=%async_computation.1 | async-start | bytes 393216 | tf_op jit(solution)/shard_map/reduce_scatter | solution.py:216
  8.7 215.7 %collective-permute-start.9 = (bf16[32,2,256]{2,0,1:T(8,128)(2,1)}, bf16[32,2,256]{2,0,1:T(8,128)(2,1)}, u32[]{:S(2)}, u32[]{:S(2)}) collective-permute-start(bf16[32,2,256]{2,0,1:T(8,128)(2,1)} %get-tuple-element.336), channel_id=1, source_target_pairs={{0,2},{2,4},{4,6},{6,8},{8,10},{10,12},{12,14},{14,16},{16,18},{18... | collective-permute-start | bytes 98312 | tf_op jit(solution)/shard_map/ppermute | solution.py:198
  11.7 214.8 %collective-permute-start.10 = (bf16[32,2,256]{2,0,1:T(8,128)(2,1)}, bf16[32,2,256]{2,0,1:T(8,128)(2,1)}, u32[]{:S(2)}, u32[]{:S(2)}) collective-permute-start(bf16[32,2,256]{2,0,1:T(8,128)(2,1)} %get-tuple-element.336), channel_id=1, source_target_pairs={{0,30},{2,0},{4,2},{6,4},{8,6},{10,8},{12,10},{14,12},{16,14},{18,... | collective-permute-start | bytes 98312 | tf_op jit(solution)/shard_map/ppermute | solution.py:206
  18.3 179.9 %collective-permute-start.32 = (f32[2,2,128]{2,1,0:T(2,128)}, f32[2,2,128]{2,1,0:T(2,128)}, u32[]{:S(2)}, u32[]{:S(2)}) collective-permute-start(f32[2,2,128]{2,1,0:T(2,128)} %get-tuple-element.352), channel_id=1, source_target_pairs={{2,0},{4,2},{6,4},{8,6},{10,8},{12,10},{14,12},{16,14},{18,16},{20... | collective-permute-start | bytes 6152 | tf_op jit(solution)/shard_map/ppermute | solution.py:14
  19.6 180.6 %collective-permute-start.33 = (f32[2,2,128]{2,1,0:T(2,128)}, f32[2,2,128]{2,1,0:T(2,128)}, u32[]{:S(2)}, u32[]{:S(2)}) collective-permute-start(f32[2,2,128]{2,1,0:T(2,128)} %get-tuple-element.352), channel_id=1, source_target_pairs={{4,0},{6,2},{8,4},{10,6},{12,8},{14,10},{16,12},{18,14},{20,16},{2... | collective-permute-start | bytes 6152 | tf_op jit(solution)/shard_map/ppermute | solution.py:14
  77.2 9.2 %collective-permute-start = (f32[2,128,128]{2,1,0:T(8,128)S(1)}, f32[2,128,128]{2,1,0:T(8,128)S(1)}, u32[]{:S(2)}, u32[]{:S(2)}) collective-permute-start(f32[2,128,128]{2,1,0:T(8,128)S(1)} %convolution_add_fusion.20), channel_id=1, source_target_pairs={{2,0},{4,2},{6,4},{8,6},{10,8},{12,10},{14,12},{16,14},{18,16},{20... | collective-permute-start | bytes 393224 | tf_op jit(solution)/shard_map/while/body/eval_jaxpr/ppermute | solution.py:14
  86.7 10.1 %collective-permute-start = (f32[2,128,128]{2,1,0:T(8,128)S(1)}, f32[2,128,128]{2,1,0:T(8,128)S(1)}, u32[]{:S(2)}, u32[]{:S(2)}) collective-permute-start(f32[2,128,128]{2,1,0:T(8,128)S(1)} %convolution_add_fusion.20), channel_id=1, source_target_pairs={{2,0},{4,2},{6,4},{8,6},{10,8},{12,10},{14,12},{16,14},{18,16},{20... | collective-permute-start | bytes 393224 | tf_op jit(solution)/shard_map/while/body/eval_jaxpr/ppermute | solution.py:14
  97.1 9.2 %collective-permute-start = (f32[2,128,128]{2,1,0:T(8,128)S(1)}, f32[2,128,128]{2,1,0:T(8,128)S(1)}, u32[]{:S(2)}, u32[]{:S(2)}) collective-permute-start(f32[2,128,128]{2,1,0:T(8,128)S(1)} %convolution_add_fusion.20), channel_id=1, source_target_pairs={{2,0},{4,2},{6,4},{8,6},{10,8},{12,10},{14,12},{16,14},{18,16},{20... | collective-permute-start | bytes 393224 | tf_op jit(solution)/shard_map/while/body/eval_jaxpr/ppermute | solution.py:14
  169.2 33.0 %collective-permute-start.34 = (f32[2,2,128]{2,1,0:T(2,128)}, f32[2,2,128]{2,1,0:T(2,128)}, u32[]{:S(2)}, u32[]{:S(2)}) collective-permute-start(f32[2,2,128]{2,1,0:T(2,128)} %get-tuple-element.352), channel_id=1, source_target_pairs={{6,0},{8,2},{10,4},{12,6},{14,8},{16,10},{18,12},{20,14},{22,16},{... | collective-permute-start | bytes 6152 | tf_op jit(solution)/shard_map/ppermute | solution.py:14
  198.2 11.2 %collective-permute-start.35 = (f32[2,2,128]{2,1,0:T(2,128)}, f32[2,2,128]{2,1,0:T(2,128)S(1)}, u32[]{:S(2)}, u32[]{:S(2)}) collective-permute-start(f32[2,2,128]{2,1,0:T(2,128)} %get-tuple-element.352), channel_id=1, source_target_pairs={{8,0},{10,2},{12,4},{14,6},{16,8},{18,10},{20,12},{22,14},{24,16},... | collective-permute-start | bytes 6152 | tf_op jit(solution)/shard_map/ppermute | solution.py:14
  200.2 13.7 %collective-permute-start.36 = (f32[2,2,128]{2,1,0:T(2,128)}, f32[2,2,128]{2,1,0:T(2,128)S(1)}, u32[]{:S(2)}, u32[]{:S(2)}) collective-permute-start(f32[2,2,128]{2,1,0:T(2,128)} %get-tuple-element.352), channel_id=1, source_target_pairs={{10,0},{12,2},{14,4},{16,6},{18,8},{20,10},{22,12},{24,14},{26,16}... | collective-permute-start | bytes 6152 | tf_op jit(solution)/shard_map/ppermute | solution.py:14
  202.2 16.7 %collective-permute-start.37 = (f32[2,2,128]{2,1,0:T(2,128)}, f32[2,2,128]{2,1,0:T(2,128)S(1)}, u32[]{:S(2)}, u32[]{:S(2)}) collective-permute-start(f32[2,2,128]{2,1,0:T(2,128)} %get-tuple-element.352), channel_id=1, source_target_pairs={{12,0},{14,2},{16,4},{18,6},{20,8},{22,10},{24,12},{26,14},{28,16}... | collective-permute-start | bytes 6152 | tf_op jit(solution)/shard_map/ppermute | solution.py:14
  209.4 12.0 %collective-permute-start.38 = (f32[2,2,128]{2,1,0:T(2,128)}, f32[2,2,128]{2,1,0:T(2,128)S(1)}, u32[]{:S(2)}, u32[]{:S(2)}) collective-permute-start(f32[2,2,128]{2,1,0:T(2,128)} %get-tuple-element.352), channel_id=1, source_target_pairs={{14,0},{16,2},{18,4},{20,6},{22,8},{24,10},{26,12},{28,14},{30,16}... | collective-permute-start | bytes 6152 | tf_op jit(solution)/shard_map/ppermute | solution.py:14
  213.9 9.1 %collective-permute-start.39 = (f32[2,2,128]{2,1,0:T(2,128)}, f32[2,2,128]{2,1,0:T(2,128)S(1)}, u32[]{:S(2)}, u32[]{:S(2)}) collective-permute-start(f32[2,2,128]{2,1,0:T(2,128)} %get-tuple-element.352), channel_id=1, source_target_pairs={{16,0},{18,2},{20,4},{22,6},{24,8},{26,10},{28,12},{30,14},{17,1},... | collective-permute-start | bytes 6152 | tf_op jit(solution)/shard_map/ppermute | solution.py:14
  218.9 40.7 %collective-permute-start.24 = (bf16[2,128,256]{1,2,0:T(8,128)(2,1)S(1)}, bf16[2,128,256]{1,2,0:T(8,128)(2,1)S(1)}, u32[]{:S(2)}, u32[]{:S(2)}) collective-permute-start(bf16[2,128,256]{1,2,0:T(8,128)(2,1)S(1)} %get-tuple-element.334), channel_id=1, source_target_pairs={{2,0},{4,2},{6,4},{8,6},{10,8},{12,10},{14,12},{16,14},{18,16},{20... | collective-permute-start | bytes 393224 | tf_op jit(solution)/shard_map/ppermute | solution.py:14
  221.4 39.5 %collective-permute-start.25 = (bf16[2,128,256]{1,2,0:T(8,128)(2,1)S(1)}, bf16[2,128,256]{1,2,0:T(8,128)(2,1)S(1)}, u32[]{:S(2)}, u32[]{:S(2)}) collective-permute-start(bf16[2,128,256]{1,2,0:T(8,128)(2,1)S(1)} %get-tuple-element.334), channel_id=1, source_target_pairs={{4,0},{6,2},{8,4},{10,6},{12,8},{14,10},{16,12},{18,14},{20,16},{2... | collective-permute-start | bytes 393224 | tf_op jit(solution)/shard_map/ppermute | solution.py:14
  223.0 39.3 %collective-permute-start.26 = (bf16[2,128,256]{1,2,0:T(8,128)(2,1)S(1)}, bf16[2,128,256]{1,2,0:T(8,128)(2,1)S(1)}, u32[]{:S(2)}, u32[]{:S(2)}) collective-permute-start(bf16[2,128,256]{1,2,0:T(8,128)(2,1)S(1)} %get-tuple-element.334), channel_id=1, source_target_pairs={{6,0},{8,2},{10,4},{12,6},{14,8},{16,10},{18,12},{20,14},{22,16},{... | collective-permute-start | bytes 393224 | tf_op jit(solution)/shard_map/ppermute | solution.py:14
  224.4 39.3 %collective-permute-start.27 = (bf16[2,128,256]{1,2,0:T(8,128)(2,1)S(1)}, bf16[2,128,256]{1,2,0:T(8,128)(2,1)S(1)}, u32[]{:S(2)}, u32[]{:S(2)}) collective-permute-start(bf16[2,128,256]{1,2,0:T(8,128)(2,1)S(1)} %get-tuple-element.334), channel_id=1, source_target_pairs={{8,0},{10,2},{12,4},{14,6},{16,8},{18,10},{20,12},{22,14},{24,16},... | collective-permute-start | bytes 393224 | tf_op jit(solution)/shard_map/ppermute | solution.py:14
  226.4 15.4 %collective-permute-start.11 = (bf16[32,2,256]{2,0,1:T(8,128)(2,1)}, bf16[32,2,256]{2,0,1:T(8,128)(2,1)S(1)}, u32[]{:S(2)}, u32[]{:S(2)}) collective-permute-start(bf16[32,2,256]{2,0,1:T(8,128)(2,1)} %collective-permute-done.9), channel_id=1, source_target_pairs={{0,2},{2,4},{4,6},{6,8},{8,10},{10,12},{12,14},{14,16},{16,18},{18... | collective-permute-start | bytes 98312 | tf_op jit(solution)/shard_map/ppermute | solution.py:198
  257.6 11.6 %collective-permute-start.28 = (bf16[2,128,256]{1,2,0:T(8,128)(2,1)S(1)}, bf16[2,128,256]{1,2,0:T(8,128)(2,1)S(1)}, u32[]{:S(2)}, u32[]{:S(2)}) collective-permute-start(bf16[2,128,256]{1,2,0:T(8,128)(2,1)S(1)} %get-tuple-element.334), channel_id=1, source_target_pairs={{10,0},{12,2},{14,4},{16,6},{18,8},{20,10},{22,12},{24,14},{26,16}... | collective-permute-start | bytes 393224 | tf_op jit(solution)/shard_map/ppermute | solution.py:14
  259.6 16.0 %collective-permute-start.29 = (bf16[2,128,256]{1,2,0:T(8,128)(2,1)S(1)}, bf16[2,128,256]{1,2,0:T(8,128)(2,1)S(1)}, u32[]{:S(2)}, u32[]{:S(2)}) collective-permute-start(bf16[2,128,256]{1,2,0:T(8,128)(2,1)S(1)} %get-tuple-element.334), channel_id=1, source_target_pairs={{12,0},{14,2},{16,4},{18,6},{20,8},{22,10},{24,12},{26,14},{28,16}... | collective-permute-start | bytes 393224 | tf_op jit(solution)/shard_map/ppermute | solution.py:14
  261.0 16.9 %collective-permute-start.30 = (bf16[2,128,256]{1,2,0:T(8,128)(2,1)S(1)}, bf16[2,128,256]{1,2,0:T(8,128)(2,1)S(1)}, u32[]{:S(2)}, u32[]{:S(2)}) collective-permute-start(bf16[2,128,256]{1,2,0:T(8,128)(2,1)S(1)} %get-tuple-element.334), channel_id=1, source_target_pairs={{14,0},{16,2},{18,4},{20,6},{22,8},{24,10},{26,12},{28,14},{30,16}... | collective-permute-start | bytes 393224 | tf_op jit(solution)/shard_map/ppermute | solution.py:14
  262.3 16.9 %collective-permute-start.31 = (bf16[2,128,256]{1,2,0:T(8,128)(2,1)S(1)}, bf16[2,128,256]{1,2,0:T(8,128)(2,1)S(1)}, u32[]{:S(2)}, u32[]{:S(2)}) collective-permute-start(bf16[2,128,256]{1,2,0:T(8,128)(2,1)S(1)} %get-tuple-element.334), channel_id=1, source_target_pairs={{16,0},{18,2},{20,4},{22,6},{24,8},{26,10},{28,12},{30,14},{17,1},... | collective-permute-start | bytes 393224 | tf_op jit(solution)/shard_map/ppermute | solution.py:14
  263.7 17.3 %collective-permute-start.1 = (bf16[2,128,256]{1,2,0:T(8,128)(2,1)}, bf16[2,128,256]{1,2,0:T(8,128)(2,1)S(1)}, u32[]{:S(2)}, u32[]{:S(2)}) collective-permute-start(bf16[2,128,256]{1,2,0:T(8,128)(2,1)} %pad_maximum_fusion), channel_id=1, source_target_pairs={{0,16},{2,18},{4,20},{6,22},{8,24},{10,26},{12,28},{14,30},{1,17},... | collective-permute-start | bytes 393224 | tf_op jit(solution)/shard_map/ppermute | solution.py:14
  269.2 15.7 %collective-permute-start.2 = (bf16[2,128,256]{1,2,0:T(8,128)(2,1)}, bf16[2,128,256]{1,2,0:T(8,128)(2,1)S(1)}, u32[]{:S(2)}, u32[]{:S(2)}) collective-permute-start(bf16[2,128,256]{1,2,0:T(8,128)(2,1)} %pad_maximum_fusion), channel_id=1, source_target_pairs={{0,14},{2,16},{4,18},{6,20},{8,22},{10,24},{12,26},{14,28},{16,30}... | collective-permute-start | bytes 393224 | tf_op jit(solution)/shard_map/ppermute | solution.py:14
  275.6 10.9 %collective-permute-start.3 = (bf16[2,128,256]{1,2,0:T(8,128)(2,1)}, bf16[2,128,256]{1,2,0:T(8,128)(2,1)S(1)}, u32[]{:S(2)}, u32[]{:S(2)}) collective-permute-start(bf16[2,128,256]{1,2,0:T(8,128)(2,1)} %pad_maximum_fusion), channel_id=1, source_target_pairs={{0,12},{2,14},{4,16},{6,18},{8,20},{10,22},{12,24},{14,26},{16,28}... | collective-permute-start | bytes 393224 | tf_op jit(solution)/shard_map/ppermute | solution.py:14
  277.9 12.2 %collective-permute-start.4 = (bf16[2,128,256]{1,2,0:T(8,128)(2,1)}, bf16[2,128,256]{1,2,0:T(8,128)(2,1)S(1)}, u32[]{:S(2)}, u32[]{:S(2)}) collective-permute-start(bf16[2,128,256]{1,2,0:T(8,128)(2,1)} %pad_maximum_fusion), channel_id=1, source_target_pairs={{0,10},{2,12},{4,14},{6,16},{8,18},{10,20},{12,22},{14,24},{16,26}... | collective-permute-start | bytes 393224 | tf_op jit(solution)/shard_map/ppermute | solution.py:14
  279.2 12.1 %collective-permute-start.5 = (bf16[2,128,256]{1,2,0:T(8,128)(2,1)}, bf16[2,128,256]{1,2,0:T(8,128)(2,1)S(1)}, u32[]{:S(2)}, u32[]{:S(2)}) collective-permute-start(bf16[2,128,256]{1,2,0:T(8,128)(2,1)} %pad_maximum_fusion), channel_id=1, source_target_pairs={{0,8},{2,10},{4,12},{6,14},{8,16},{10,18},{12,20},{14,22},{16,24},... | collective-permute-start | bytes 393224 | tf_op jit(solution)/shard_map/ppermute | solution.py:14
  281.0 14.9 %collective-permute-start.6 = (bf16[2,128,256]{1,2,0:T(8,128)(2,1)}, bf16[2,128,256]{1,2,0:T(8,128)(2,1)S(1)}, u32[]{:S(2)}, u32[]{:S(2)}) collective-permute-start(bf16[2,128,256]{1,2,0:T(8,128)(2,1)} %pad_maximum_fusion), channel_id=1, source_target_pairs={{0,6},{2,8},{4,10},{6,12},{8,14},{10,16},{12,18},{14,20},{16,22},{... | collective-permute-start | bytes 393224 | tf_op jit(solution)/shard_map/ppermute | solution.py:14
  284.9 11.0 %collective-permute-start.7 = (bf16[2,128,256]{1,2,0:T(8,128)(2,1)}, bf16[2,128,256]{1,2,0:T(8,128)(2,1)S(1)}, u32[]{:S(2)}, u32[]{:S(2)}) collective-permute-start(bf16[2,128,256]{1,2,0:T(8,128)(2,1)} %pad_maximum_fusion), channel_id=1, source_target_pairs={{0,4},{2,6},{4,8},{6,10},{8,12},{10,14},{12,16},{14,18},{16,20},{1... | collective-permute-start | bytes 393224 | tf_op jit(solution)/shard_map/ppermute | solution.py:14
  286.5 9.4 %collective-permute-start.8 = (bf16[2,128,256]{1,2,0:T(8,128)(2,1)}, bf16[2,128,256]{1,2,0:T(8,128)(2,1)S(1)}, u32[]{:S(2)}, u32[]{:S(2)}) collective-permute-start(bf16[2,128,256]{1,2,0:T(8,128)(2,1)} %pad_maximum_fusion), channel_id=1, source_target_pairs={{0,2},{2,4},{4,6},{6,8},{8,10},{10,12},{12,14},{14,16},{16,18},{18... | collective-permute-start | bytes 393224 | tf_op jit(solution)/shard_map/ppermute | solution.py:14
  290.0 10.1 %collective-permute-start.15 = (bf16[32,2,256]{2,0,1:T(8,128)(2,1)}, bf16[32,2,256]{2,0,1:T(8,128)(2,1)}, u32[]{:S(2)}, u32[]{:S(2)}) collective-permute-start(bf16[32,2,256]{2,0,1:T(8,128)(2,1)} %collective-permute-done.13), channel_id=1, source_target_pairs={{0,2},{2,4},{4,6},{6,8},{8,10},{10,12},{12,14},{14,16},{16,18},{18... | collective-permute-start | bytes 98312 | tf_op jit(solution)/shard_map/ppermute | solution.py:198
  (86 other events, 558.7 us)
Sparse Core Ops, SparseCore 0:
  331.7 3.5 reduce-scatter.1
